TPU v7x, 32 devices: a whole 2x2x4 slice. The times are simulated.
32 devices in a mesh: space: 2 (over y), chaos: 16 (over z, x, core).
Axes of the slice: x: 2, y: 2, z: 4, core: 2. Of those that a mesh axis runs over, the one named last changes fastest.
Arguments:
- kl_fields: float32 [9, 4, 16, 512], P(None, None, 'space'), may hold values from -5 to 5
- labels: int32 [4, 16, 512], P(None, 'space'), may hold values from 0 to 3
- region_scale: float32 [4, 9], replicated, may hold values from 0.5 to 2
- background: float32 [4, 16, 512], P(None, 'space'), may hold values from -4 to 4
- galerkin_table: int32 [384, 3], replicated, may hold values from 0 to 47, as said below
- triple_values: float32 [384], replicated, may hold values from -4 to 4
- direction: float32 [48, 3, 4, 16, 512], P('chaos', None, None, 'space'), may hold values from -6 to 6
Outputs:
- result: float32 [48, 3, 4, 16, 512], P('chaos', None, None, 'space')
Inputs may be any that keep to these rules, and one draw needn't show every extreme that they name: `galerkin_table`: row r has term i = r // 8; the first row of each term is (i, i, 0); the others name any term j and a mode k of 1 to 8.
All inputs are finite; a program needn't handle non-finite values.
Results may differ from a plain program's by a relative error of at most 0.000076.
Values sent between devices are 32-bit elements; how exact they have to be, the bound alone decides.
A program may use at most 128 MiB of HBM per device.

v0:
```python
import jax
import jax.numpy as jnp
from jax import lax
from jax.sharding import PartitionSpec as P


def extended(array, sides, width):
    for axis, dim in sides:
        size, length = (lax.axis_size(axis), array.shape[dim])
        up = [(i, (i + 1) % size) for i in range(size - 1)]
        down = [(j, i) for i, j in up]
        last = lax.slice_in_dim(array, length - width, length, axis=dim)
        initial = lax.slice_in_dim(array, 0, width, axis=dim)
        before = lax.ppermute(last, axis, up)
        after = lax.ppermute(initial, axis, down)
        array = jnp.concatenate([before, array, after], axis=dim)
    return array


def neighbours(padded):
    middle = padded[..., 1:-1, :]
    row_next = padded[..., 2:, :]
    row_prev = padded[..., :-2, :]
    plane_zero = jnp.zeros_like(middle[..., :1, :, :])
    plane_next = jnp.concatenate([middle[..., 1:, :, :], plane_zero], axis=-3)
    plane_prev = jnp.concatenate([plane_zero, middle[..., :-1, :, :]], axis=-3)
    column_zero = jnp.zeros_like(middle[..., :1])
    column_next = jnp.concatenate([middle[..., 1:], column_zero], axis=-1)
    column_prev = jnp.concatenate([column_zero, middle[..., :-1]], axis=-1)
    return (middle, (row_next, row_prev, plane_next, plane_prev, column_next, column_prev))


def drift_terms(potential_pad):
    middle, beside_all = neighbours(potential_pad)
    return tuple((0.5 * (other - middle) for other in beside_all))


def jacobian_block(coef_pad, potential_pad, electron_pad, hole_pad, drift_list):
    coef_mid, coef_nbr = neighbours(coef_pad)
    pot_mid, pot_nbr = neighbours(potential_pad)
    ele_mid, ele_nbr = neighbours(electron_pad)
    hole_mid, hole_nbr = neighbours(hole_pad)
    out_potential = coef_mid * (ele_mid - hole_mid)
    out_electron = jnp.zeros_like(out_potential)
    out_holes = jnp.zeros_like(out_potential)
    for facing in range(6):
        conduct = 0.5 * (coef_mid + coef_nbr[facing])
        potential_rise = pot_nbr[facing] - pot_mid
        drift_now = drift_list[facing]
        out_potential = out_potential - conduct * potential_rise
        out_electron = out_electron + conduct * (
            ele_mid - ele_nbr[facing] - drift_now * (ele_mid + ele_nbr[facing]) - potential_rise
        )
        out_holes = out_holes + conduct * (
            hole_mid - hole_nbr[facing] + drift_now * (hole_mid + hole_nbr[facing]) + potential_rise
        )
    return jnp.stack([out_potential, out_electron, out_holes], axis=-4)


def shards(kl_fields, labels, region_scale, background, galerkin_table, triple_values, direction):
    term_dev = direction.shape[0]
    group_count = lax.axis_size("chaos")
    all_terms = term_dev * group_count
    first_term = lax.axis_index("chaos") * term_dev
    region_count = region_scale.shape[0]
    mode_count = region_scale.shape[1]
    lookup = jnp.zeros(kl_fields.shape, jnp.float32)
    for region in range(region_count):
        lookup = (
            lookup
            + (labels == region).astype(jnp.float32)[None]
            * region_scale[region][:, None, None, None]
        )
    scaled = kl_fields * lookup
    stacked = jnp.concatenate([scaled, background[None]], axis=0)
    rimmed = extended(stacked, (("space", 2),), 1)
    coef_pad = rimmed[:-1]
    drift_list = drift_terms(rimmed[-1])
    local_hot = (
        galerkin_table[:, 0][:, None] == first_term + jnp.arange(term_dev, dtype=jnp.int32)[None]
    ).astype(jnp.float32)
    source_hot = (
        galerkin_table[:, 1][:, None] == jnp.arange(all_terms, dtype=jnp.int32)[None]
    ).astype(jnp.float32)
    mode_hot = (
        galerkin_table[:, 2][:, None] == jnp.arange(mode_count, dtype=jnp.int32)[None]
    ).astype(jnp.float32)
    mixing = jnp.einsum(
        "t,ta,tj,tk->ajk",
        triple_values,
        local_hot,
        source_hot,
        mode_hot,
        precision=lax.Precision.HIGHEST,
    )
    zeros_out = jnp.zeros(direction.shape, jnp.float32)
    own_pad = extended(direction, (("space", 3),), 1)
    term_block = lax.all_gather(own_pad, "chaos", axis=0, tiled=True)
    block_terms = term_block.shape[0]

    def one_pair(pair_index, total):
        target = pair_index // block_terms
        source = pair_index % block_terms
        pair_weights = mixing[target, source]

        def apply_pair(unused):
            pair_coef = jnp.einsum(
                "k,kprc->prc", pair_weights, coef_pad, precision=lax.Precision.HIGHEST
            )
            fields = lax.dynamic_index_in_dim(term_block, source, 0, keepdims=False)
            return jacobian_block(pair_coef, fields[0], fields[1], fields[2], drift_list)

        def skip_pair(unused):
            return jnp.zeros(direction.shape[1:], jnp.float32)

        update = lax.cond(jnp.any(pair_weights != 0.0), apply_pair, skip_pair, 0)
        current = lax.dynamic_index_in_dim(total, target, 0, keepdims=False)
        return lax.dynamic_update_index_in_dim(total, current + update, target, 0)

    return lax.fori_loop(0, term_dev * block_terms, one_pair, zeros_out)


def solution(mesh):
    return jax.shard_map(
        shards,
        mesh=mesh,
        in_specs=(
            P(None, None, "space", None),
            P(None, "space", None),
            P(),
            P(None, "space", None),
            P(),
            P(),
            P("chaos", None, None, "space", None),
        ),
        out_specs=P("chaos", None, None, "space", None),
        check_vma=False,
    )
```

profile of v0, /device:TPU:0, one launch (start us, length us, event | category | flops | bytes accessed | tf_op | source)
XLA Modules:
  0.0 422.6 jit_solution(8876589187335992419)
XLA Ops:
  6.5 1.4 copy.9
  8.0 5.0 %collective-permute-start.2 = (f32[3,3,4,1,512]{4,2,3,1,0:T(4,128)S(1)}, f32[3,3,4,1,512]{4,2,3,1,0:T(4,128)S(1)}, u32[]{:S(2)}, u32[]{:S(2)}) collective-permute-start(f32[3,3,4,1,512]{4,2,3,1,0:T(4,128)S(1)} %get-tuple-element.391), channel_id=1, source_target_pairs={{0,16},{1,17},{2,18},{3,19},{4,20},{5,21},{6,22},{7,23},{8,24},{9,... | collective-permute-start | bytes 221192 | tf_op jit(solution)/shard_map/ppermute | solution.py:14
  13.1 1.3 collective-permute-start.3
  15.0 4.3 %collective-permute-done.3 = f32[3,3,4,1,512]{4,2,3,1,0:T(4,128)S(1)} collective-permute-done((f32[3,3,4,1,512]{4,2,3,1,0:T(4,128)S(1)}, f32[3,3,4,1,512]{4,2,3,1,0:T(4,128)S(1)}, u32[]{:S(2)}, u32[]{:S(2)}) %collective-permute-start.3) | collective-permute-done | bytes 73760 | tf_op jit(solution)/shard_map/ppermute | solution.py:15
  21.4 1.6 collective-permute-start
  25.0 4.3 %collective-permute-done.1 = f32[10,4,1,512]{3,2,1,0:T(1,128)S(1)} collective-permute-done((f32[10,4,1,512]{3,2,1,0:T(1,128)S(1)}, f32[10,4,1,512]{3,2,1,0:T(1,128)S(1)}, u32[]{:S(2)}, u32[]{:S(2)}) %collective-permute-start.1) | collective-permute-done | bytes 81952 | tf_op jit(solution)/shard_map/ppermute | solution.py:15
  29.9 86.6 %all-gather.2.cloned.1.call-done = f32[48,3,4,10,512]{4,2,3,1,0:T(4,128)} async-done(((f32[3,3,4,10,512]{4,2,3,1,0:T(4,128)}), f32[48,3,4,10,512]{4,2,3,1,0:T(4,128)}) %all-gather.2.cloned.1.call-update) | async-done | bytes 11796496 | tf_op jit(solution)/shard_map/all_gather | solution.py:98
  116.5 17.0 %copy.13 = f32[48,3,4,10,512]{4,3,2,1,0:T(8,128)} copy(f32[48,3,4,10,512]{4,2,3,1,0:T(4,128)} %all-gather.2.cloned.1.call-done) | data formatting | bytes 23592960 | tf_op jit(solution)/shard_map/while | solution.py:120
  133.5 281.4 %while.15 = (s32[]{:T(128)}, f32[3,3,4,8,512]{4,3,2,1,0:T(8,128)S(1)}, f32[3,48,9]{2,1,0:T(8,128)S(1)}, f32[9,4,10,512]{3,2,1,0:T(8,128)S(1)}, f32[48,3,4,10,512...) while((s32[]{:T(128)}, ...), condition=%wide.region_4.5_spmd, body=%wide.region_0.4_spmd.sunk | while | flops 4816939 | bytes 9204332 | solution.py:120
  134.9 3.1 conditional.2
  157.0 3.1 conditional.2
  173.3 3.1 conditional.2
  188.1 3.1 conditional.2
  194.1 3.1 conditional.2
  198.5 3.1 conditional.2
  211.9 3.1 conditional.2
  217.8 3.1 conditional.2
  231.2 3.1 conditional.2
  240.1 3.1 conditional.2
  249.0 3.1 conditional.2
  265.2 3.1 conditional.2
  272.7 3.1 conditional.2
  303.7 3.1 conditional.2
  309.6 3.1 conditional.2
  314.1 3.1 conditional.2
  327.4 3.1 conditional.2
  333.4 3.1 conditional.2
  342.3 3.1 conditional.2
  361.5 3.1 conditional.2
  391.0 3.1 conditional.2
  395.5 3.1 conditional.2
  408.8 3.1 conditional.2
  (965 shorter events, 184.7 us)
Async XLA Ops:
  6.5 109.9 %all-gather.2.cloned.1.call-start = ((), (), s32[]{:S(2)}) async-start(), calls=%async_computation | async-start | bytes 12533760 | tf_op jit(solution)/shard_map/all_gather | solution.py:98
  8.0 12.5 %copy-start.5 = (f32[4,9]{1,0:T(4,128)S(1)}, f32[4,9]{1,0:T(4,128)}, u32[]{:S(2)}) copy-start(f32[4,9]{1,0:T(4,128)} %param.13) | copy-start | bytes 436
  8.0 12.5 %copy-start.3 = (s32[4,8,512]{2,1,0:T(8,128)S(1)}, s32[4,8,512]{2,1,0:T(8,128)}, u32[]{:S(2)}) copy-start(s32[4,8,512]{2,1,0:T(8,128)} %param.12) | copy-start | bytes 196612
  8.0 12.5 %copy-start.1 = (f32[9,4,8,512]{3,2,1,0:T(8,128)S(1)}, f32[9,4,8,512]{3,2,1,0:T(8,128)}, u32[]{:S(2)}) copy-start(f32[9,4,8,512]{3,2,1,0:T(8,128)} %param.11) | copy-start | bytes 1769476
  8.0 7.0 %collective-permute-start.2 = (f32[3,3,4,1,512]{4,2,3,1,0:T(4,128)S(1)}, f32[3,3,4,1,512]{4,2,3,1,0:T(4,128)S(1)}, u32[]{:S(2)}, u32[]{:S(2)}) collective-permute-start(f32[3,3,4,1,512]{4,2,3,1,0:T(4,128)S(1)} %get-tuple-element.391), channel_id=1, source_target_pairs={{0,16},{1,17},{2,18},{3,19},{4,20},{5,21},{6,22},{7,23},{8,24},{9,... | collective-permute-start | bytes 221192 | tf_op jit(solution)/shard_map/ppermute | solution.py:14
  13.1 6.2 %collective-permute-start.3 = (f32[3,3,4,1,512]{4,2,3,1,0:T(4,128)S(1)}, f32[3,3,4,1,512]{4,2,3,1,0:T(4,128)S(1)}, u32[]{:S(2)}, u32[]{:S(2)}) collective-permute-start(f32[3,3,4,1,512]{4,2,3,1,0:T(4,128)S(1)} %get-tuple-element.392), channel_id=1, source_target_pairs={{16,0},{17,1},{18,2},{19,3},{20,4},{21,5},{22,6},{23,7},{24,8},{25... | collective-permute-start | bytes 221192 | tf_op jit(solution)/shard_map/ppermute | solution.py:15
  20.4 0.8 copy-start.2
  20.5 3.8 copy-start.4
  20.5 3.8 copy-start.6
  21.4 3.6 collective-permute-start
  22.9 6.3 %collective-permute-start.1 = (f32[10,4,1,512]{3,2,1,0:T(1,128)S(1)}, f32[10,4,1,512]{3,2,1,0:T(1,128)S(1)}, u32[]{:S(2)}, u32[]{:S(2)}) collective-permute-start(f32[10,4,1,512]{3,2,1,0:T(1,128)S(1)} %get-tuple-element.390), channel_id=1, source_target_pairs={{16,0},{17,1},{18,2},{19,3},{20,4},{21,5},{22,6},{23,7},{24,8},{25... | collective-permute-start | bytes 245768 | tf_op jit(solution)/shard_map/ppermute | solution.py:15
  414.9 0.8 copy-start
Sparse Core Ops, SparseCore 0:
  20.6 95.8 all-gather.1
where the time goes:
time: 425 us; the launch traced here: 423 us
  other arithmetic  114 us (27%)
  loops' own time  107 us (25%)
  waiting for transfers between devices  96.2 us (23%)
  local copies, waits for them, and re-layouts  55.7 us (13%)
  matrix products  26.4 us (6%)
  between operations  13.6 us (3%)
  starting transfers between devices  9.18 us (2%)
    another operation x1, loops' own time, shards(): return lax.fori_loop(0, term_dev * block_terms, one_pair, zeros_out)  102 us
    reduce_or x144, other arithmetic, one_pair(): update = lax.cond(jnp.any(pair_weights != 0.0), apply_pair, skip_pair, 0)  96.1 us
    all_gather x1, waiting for transfers between devices, shards(): term_block = lax.all_gather(own_pad, 'chaos', axis=0, tiled=True)  86.6 us
    dot_general x23, matrix products, apply_pair(): jnp.einsum('k,kprc->prc', pair_weights, coef_pad, precision=lax.Precision...  26.2 us
    squeeze x23, local copies, waits for them, and re-layouts, apply_pair(): fields[1]  24.5 us
    while x2, local copies, waits for them, and re-layouts, shards(): return lax.fori_loop(0, term_dev * block_terms, one_pair, zeros_out)  17.1 us
    another operation x92, other arithmetic, jacobian_block(): return jnp.stack([out_potential, out_electron, out_holes], axis=-4)  11.4 us
    ppermute x2, waiting for transfers between devices, extended(): after = lax.ppermute(initial, axis, down)  8.58 us
  transfers between devices with their start and end apart: 5, of which 5 were waited for; matrix products, arithmetic and copies ran while one was open for 0% of the time, Pallas kernels for 0%

commit v1 on v0

--- a/solution.py
+++ b/solution.py
@@ -95,7 +95,14 @@
     )
     zeros_out = jnp.zeros(direction.shape, jnp.float32)
     own_pad = extended(direction, (("space", 3),), 1)
-    term_block = lax.all_gather(own_pad, "chaos", axis=0, tiled=True)
+    ring = [own_pad]
+    for hop in range(15):
+        ring.append(lax.ppermute(ring[-1], "chaos", [(dev, (dev + 1) % 16) for dev in range(16)]))
+    term_block = jnp.roll(
+        jnp.concatenate(ring[::-1], axis=0),
+        (lax.axis_index("chaos") + 1) * ring[0].shape[0],
+        axis=0,
+    )
     block_terms = term_block.shape[0]
 
     def one_pair(pair_index, total):

time: 425 us -> 538 us (1.27)
  waiting for transfers between devices: 96.2 us -> 198 us
  local copies, waits for them, and re-layouts: 55.7 us -> 89.4 us
  between operations: 13.6 us -> 0.58 us
  loops' own time: 107 us -> 96.5 us
    ppermute x0 -> x15, waiting for transfers between devices: none -> 193 us  [shards(): lax.ppermute(ring[-1], 'chaos', [(dev, (dev + 1) % 16) for dev in range(1...]
    all_gather x1 -> x0, waiting for transfers between devices: 86.6 us -> none  [shards(): term_block = lax.all_gather(own_pad, 'chaos', axis=0, tiled=True)]
    unnamed x15 -> x78, local copies, waits for them, and re-layouts: 2.72 us -> 29 us
    another operation x1, loops' own time: 102 us -> 91.9 us  [shards(): return lax.fori_loop(0, term_dev * block_terms, one_pair, zeros_out)]
    dynamic_slice x0 -> x1, local copies, waits for them, and re-layouts: none -> 5.84 us  [shards(): jnp.roll(jnp.concatenate(ring[::-1], axis=0), (lax.axis_index('chaos') +...]
  transfers between devices with their start and end apart: 5 -> 19, of which waited for: 5 -> 17; matrix products, arithmetic and copies ran while one was open for 0% -> 2% of each run, Pallas kernels for 0% -> 0%
where the time goes in v1:
time: 538 us; the launch traced here: 535 us
  waiting for transfers between devices  198 us (37%)
  other arithmetic  115 us (21%)
  loops' own time  96.5 us (18%)
  local copies, waits for them, and re-layouts  89.4 us (17%)
  matrix products  26.4 us (5%)
  starting transfers between devices  9.15 us (2%)
    ppermute x15, waiting for transfers between devices, shards(): lax.ppermute(ring[-1], 'chaos', [(dev, (dev + 1) % 16) for dev in range(1...  193 us
    reduce_or x144, other arithmetic, one_pair(): update = lax.cond(jnp.any(pair_weights != 0.0), apply_pair, skip_pair, 0)  91.9 us
    another operation x1, loops' own time, shards(): return lax.fori_loop(0, term_dev * block_terms, one_pair, zeros_out)  91.9 us
    unnamed x78, local copies, waits for them, and re-layouts  29 us
    dot_general x23, matrix products, apply_pair(): jnp.einsum('k,kprc->prc', pair_weights, coef_pad, precision=lax.Precision...  26.2 us
    squeeze x23, local copies, waits for them, and re-layouts, apply_pair(): fields[1]  24.5 us
    while x2, local copies, waits for them, and re-layouts, shards(): return lax.fori_loop(0, term_dev * block_terms, one_pair, zeros_out)  17.1 us
    another operation x92, other arithmetic, jacobian_block(): return jnp.stack([out_potential, out_electron, out_holes], axis=-4)  11.4 us
  transfers between devices with their start and end apart: 19, of which 17 were waited for; matrix products, arithmetic and copies ran while one was open for 2% of the time, Pallas kernels for 0%

profile of v1, /device:TPU:0, one launch (start us, length us, event | category | flops | bytes accessed | tf_op | source)
XLA Modules:
  0.0 534.9 jit_solution(3338871598042309790)
XLA Ops:
  1.5 4.9 collective-permute-start.2
  8.4 4.3 collective-permute-done.3
  13.0 13.6 %collective-permute-done.4 = f32[3,3,4,10,512]{4,2,3,1,0:T(4,128)S(1)} collective-permute-done((f32[3,3,4,10,512]{4,2,3,1,0:T(4,128)S(1)}, f32[3,3,4,10,512]{4,2,3,1,0:T(4,128)S(1)}, u32[]{:S(2)}, u32[]{:S(2)}) %collective-permute-start.4) | collective-permute-done | bytes 737312 | tf_op jit(solution)/shard_map/ppermute | solution.py:100
  26.5 13.6 %collective-permute-done.5 = f32[3,3,4,10,512]{4,2,3,1,0:T(4,128)S(1)} collective-permute-done((f32[3,3,4,10,512]{4,2,3,1,0:T(4,128)S(1)}, f32[3,3,4,10,512]{4,2,3,1,0:T(4,128)S(1)}, u32[]{:S(2)}, u32[]{:S(2)}) %collective-permute-start.5) | collective-permute-done | bytes 737312 | tf_op jit(solution)/shard_map/ppermute | solution.py:100
  40.1 13.6 %collective-permute-done.6 = f32[3,3,4,10,512]{4,2,3,1,0:T(4,128)S(1)} collective-permute-done((f32[3,3,4,10,512]{4,2,3,1,0:T(4,128)S(1)}, f32[3,3,4,10,512]{4,2,3,1,0:T(4,128)S(1)}, u32[]{:S(2)}, u32[]{:S(2)}) %collective-permute-start.6) | collective-permute-done | bytes 737312 | tf_op jit(solution)/shard_map/ppermute | solution.py:100
  54.6 13.6 %collective-permute-done.7 = f32[3,3,4,10,512]{4,2,3,1,0:T(4,128)S(1)} collective-permute-done((f32[3,3,4,10,512]{4,2,3,1,0:T(4,128)S(1)}, f32[3,3,4,10,512]{4,2,3,1,0:T(4,128)S(1)}, u32[]{:S(2)}, u32[]{:S(2)}) %collective-permute-start.7) | collective-permute-done | bytes 737312 | tf_op jit(solution)/shard_map/ppermute | solution.py:100
  69.1 13.6 %collective-permute-done.8 = f32[3,3,4,10,512]{4,2,3,1,0:T(4,128)S(1)} collective-permute-done((f32[3,3,4,10,512]{4,2,3,1,0:T(4,128)S(1)}, f32[3,3,4,10,512]{4,2,3,1,0:T(4,128)S(1)}, u32[]{:S(2)}, u32[]{:S(2)}) %collective-permute-start.8) | collective-permute-done | bytes 737312 | tf_op jit(solution)/shard_map/ppermute | solution.py:100
  82.7 13.6 %collective-permute-done.9 = f32[3,3,4,10,512]{4,2,3,1,0:T(4,128)S(1)} collective-permute-done((f32[3,3,4,10,512]{4,2,3,1,0:T(4,128)S(1)}, f32[3,3,4,10,512]{4,2,3,1,0:T(4,128)S(1)}, u32[]{:S(2)}, u32[]{:S(2)}) %collective-permute-start.9) | collective-permute-done | bytes 737312 | tf_op jit(solution)/shard_map/ppermute | solution.py:100
  97.1 13.6 %collective-permute-done.10 = f32[3,3,4,10,512]{4,2,3,1,0:T(4,128)S(1)} collective-permute-done((f32[3,3,4,10,512]{4,2,3,1,0:T(4,128)S(1)}, f32[3,3,4,10,512]{4,2,3,1,0:T(4,128)S(1)}, u32[]{:S(2)}, u32[]{:S(2)}) %collective-permute-start.10) | collective-permute-done | bytes 737312 | tf_op jit(solution)/shard_map/ppermute | solution.py:100
  111.6 13.6 %collective-permute-done.11 = f32[3,3,4,10,512]{4,2,3,1,0:T(4,128)S(1)} collective-permute-done((f32[3,3,4,10,512]{4,2,3,1,0:T(4,128)S(1)}, f32[3,3,4,10,512]{4,2,3,1,0:T(4,128)S(1)}, u32[]{:S(2)}, u32[]{:S(2)}) %collective-permute-start.11) | collective-permute-done | bytes 737312 | tf_op jit(solution)/shard_map/ppermute | solution.py:100
  126.0 13.6 %collective-permute-done.12 = f32[3,3,4,10,512]{4,2,3,1,0:T(4,128)S(1)} collective-permute-done((f32[3,3,4,10,512]{4,2,3,1,0:T(4,128)S(1)}, f32[3,3,4,10,512]{4,2,3,1,0:T(4,128)S(1)}, u32[]{:S(2)}, u32[]{:S(2)}) %collective-permute-start.12) | collective-permute-done | bytes 737312 | tf_op jit(solution)/shard_map/ppermute | solution.py:100
  140.5 13.6 %collective-permute-done.13 = f32[3,3,4,10,512]{4,2,3,1,0:T(4,128)S(1)} collective-permute-done((f32[3,3,4,10,512]{4,2,3,1,0:T(4,128)S(1)}, f32[3,3,4,10,512]{4,2,3,1,0:T(4,128)S(1)}, u32[]{:S(2)}, u32[]{:S(2)}) %collective-permute-start.13) | collective-permute-done | bytes 737312 | tf_op jit(solution)/shard_map/ppermute | solution.py:100
  155.0 13.6 %collective-permute-done.14 = f32[3,3,4,10,512]{4,2,3,1,0:T(4,128)S(1)} collective-permute-done((f32[3,3,4,10,512]{4,2,3,1,0:T(4,128)S(1)}, f32[3,3,4,10,512]{4,2,3,1,0:T(4,128)S(1)}, u32[]{:S(2)}, u32[]{:S(2)}) %collective-permute-start.14) | collective-permute-done | bytes 737312 | tf_op jit(solution)/shard_map/ppermute | solution.py:100
  169.5 12.8 %collective-permute-done.15 = f32[3,3,4,10,512]{4,2,3,1,0:T(4,128)} collective-permute-done((f32[3,3,4,10,512]{4,2,3,1,0:T(4,128)S(1)}, f32[3,3,4,10,512]{4,2,3,1,0:T(4,128)}, u32[]{:S(2)}, u32[]{:S(2)}) %collective-permute-start.15) | collective-permute-done | bytes 737312 | tf_op jit(solution)/shard_map/ppermute | solution.py:100
  189.2 7.0 %collective-permute-done.16 = f32[3,3,4,10,512]{4,2,3,1,0:T(4,128)} collective-permute-done((f32[3,3,4,10,512]{4,2,3,1,0:T(4,128)}, f32[3,3,4,10,512]{4,2,3,1,0:T(4,128)}, u32[]{:S(2)}, u32[]{:S(2)}) %collective-permute-start.16) | collective-permute-done | bytes 737312 | tf_op jit(solution)/shard_map/ppermute | solution.py:100
  198.5 11.5 %collective-permute-done.17 = f32[3,3,4,10,512]{4,2,3,1,0:T(4,128)} collective-permute-done((f32[3,3,4,10,512]{4,2,3,1,0:T(4,128)}, f32[3,3,4,10,512]{4,2,3,1,0:T(4,128)}, u32[]{:S(2)}, u32[]{:S(2)}) %collective-permute-start.17) | collective-permute-done | bytes 737312 | tf_op jit(solution)/shard_map/ppermute | solution.py:100
  211.3 12.6 %collective-permute-done.18 = f32[3,3,4,10,512]{4,2,3,1,0:T(4,128)S(1)} collective-permute-done((f32[3,3,4,10,512]{4,2,3,1,0:T(4,128)}, f32[3,3,4,10,512]{4,2,3,1,0:T(4,128)S(1)}, u32[]{:S(2)}, u32[]{:S(2)}) %collective-permute-start.18) | collective-permute-done | bytes 737312 | tf_op jit(solution)/shard_map/ppermute | solution.py:100
  244.6 5.8 %constant_dynamic-slice_fusion.2 = f32[48,3,4,10,512]{4,2,3,1,0:T(4,128)} fusion(f32[96,3,4,10,512]{4,2,3,1,0:T(4,128)S(1)} %constant_dynamic-update-slice_fusion, s32[]{:T(128)S(6)} %select_n.74), kind=kLoop, calls=%fused_computation.135 | loop fusion | bytes 23592964 | tf_op jit(solution)/shard_map/jit(_roll_dynamic)/dynamic_slice | solution.py:101
  250.5 17.0 %copy.13 = f32[48,3,4,10,512]{4,3,2,1,0:T(8,128)} copy(f32[48,3,4,10,512]{4,2,3,1,0:T(4,128)} %constant_dynamic-slice_fusion.2) | data formatting | bytes 23592960 | tf_op jit(solution)/shard_map/while | solution.py:127
  267.5 266.6 %while.15 = (s32[]{:T(128)}, f32[3,3,4,8,512]{4,3,2,1,0:T(8,128)S(1)}, f32[3,48,9]{2,1,0:T(8,128)S(1)}, f32[9,4,10,512]{3,2,1,0:T(8,128)S(1)}, f32[48,3,4,10,512...) while((s32[]{:T(128)}, ...), condition=%wide.region_4.5_spmd, body=%wide.region_0.4_spmd.sunk | while | flops 4816939 | bytes 9204332 | solution.py:127
  268.7 3.1 conditional.2
  289.6 3.1 conditional.2
  318.9 3.1 conditional.2
  329.0 3.1 conditional.2
  360.0 3.1 conditional.2
  368.5 3.1 conditional.2
  377.0 3.1 conditional.2
  392.3 3.1 conditional.2
  428.5 3.1 conditional.2
  438.6 3.1 conditional.2
  483.6 3.1 conditional.2
  528.2 3.1 conditional.2
  (1057 shorter events, 250.5 us)
Async XLA Ops:
  0.0 237.6 %copy-start = (f32[3,3,4,8,512]{4,3,2,1,0:T(8,128)S(1)}, f32[3,3,4,8,512]{4,3,2,1,0:T(8,128)}, u32[]{:S(2)}) copy-start(f32[3,3,4,8,512]{4,3,2,1,0:T(8,128)} %param.17) | copy-start | bytes 1769476
  1.5 6.9 %collective-permute-start.2 = (f32[3,3,4,1,512]{4,2,3,1,0:T(4,128)S(1)}, f32[3,3,4,1,512]{4,2,3,1,0:T(4,128)S(1)}, u32[]{:S(2)}, u32[]{:S(2)}) collective-permute-start(f32[3,3,4,1,512]{4,2,3,1,0:T(4,128)S(1)} %get-tuple-element.391), channel_id=1, source_target_pairs={{0,16},{1,17},{2,18},{3,19},{4,20},{5,21},{6,22},{7,23},{8,24},{9,... | collective-permute-start | bytes 221192 | tf_op jit(solution)/shard_map/ppermute | solution.py:14
  6.5 6.2 %collective-permute-start.3 = (f32[3,3,4,1,512]{4,2,3,1,0:T(4,128)S(1)}, f32[3,3,4,1,512]{4,2,3,1,0:T(4,128)S(1)}, u32[]{:S(2)}, u32[]{:S(2)}) collective-permute-start(f32[3,3,4,1,512]{4,2,3,1,0:T(4,128)S(1)} %get-tuple-element.392), channel_id=1, source_target_pairs={{16,0},{17,1},{18,2},{19,3},{20,4},{21,5},{22,6},{23,7},{24,8},{25... | collective-permute-start | bytes 221192 | tf_op jit(solution)/shard_map/ppermute | solution.py:15
  12.9 13.6 %collective-permute-start.4 = (f32[3,3,4,10,512]{4,2,3,1,0:T(4,128)S(1)}, f32[3,3,4,10,512]{4,2,3,1,0:T(4,128)S(1)}, u32[]{:S(2)}, u32[]{:S(2)}) collective-permute-start(f32[3,3,4,10,512]{4,2,3,1,0:T(4,128)S(1)} %pad_maximum_fusion.2), channel_id=1, source_target_pairs={{0,1},{1,2},{2,3},{3,4},{4,5},{5,6},{6,7},{7,8},{8,9},{9,10},{10,1... | collective-permute-start | bytes 2211848 | tf_op jit(solution)/shard_map/ppermute | solution.py:100
  26.5 13.6 %collective-permute-start.5 = (f32[3,3,4,10,512]{4,2,3,1,0:T(4,128)S(1)}, f32[3,3,4,10,512]{4,2,3,1,0:T(4,128)S(1)}, u32[]{:S(2)}, u32[]{:S(2)}) collective-permute-start(f32[3,3,4,10,512]{4,2,3,1,0:T(4,128)S(1)} %collective-permute-done.4), channel_id=1, source_target_pairs={{0,1},{1,2},{2,3},{3,4},{4,5},{5,6},{6,7},{7,8},{8,9},{9,10},{10,1... | collective-permute-start | bytes 2211848 | tf_op jit(solution)/shard_map/ppermute | solution.py:100
  40.1 142.9 %copy-start.2 = (f32[3,3,4,10,512]{4,2,3,1,0:T(4,128)}, f32[3,3,4,10,512]{4,2,3,1,0:T(4,128)S(1)}, u32[]{:S(2)}) copy-start(f32[3,3,4,10,512]{4,2,3,1,0:T(4,128)S(1)} %collective-permute-done.5) | copy-start | bytes 2211844
  40.1 13.6 %collective-permute-start.6 = (f32[3,3,4,10,512]{4,2,3,1,0:T(4,128)S(1)}, f32[3,3,4,10,512]{4,2,3,1,0:T(4,128)S(1)}, u32[]{:S(2)}, u32[]{:S(2)}) collective-permute-start(f32[3,3,4,10,512]{4,2,3,1,0:T(4,128)S(1)} %collective-permute-done.5), channel_id=1, source_target_pairs={{0,1},{1,2},{2,3},{3,4},{4,5},{5,6},{6,7},{7,8},{8,9},{9,10},{10,1... | collective-permute-start | bytes 2211848 | tf_op jit(solution)/shard_map/ppermute | solution.py:100
  54.6 13.6 %collective-permute-start.7 = (f32[3,3,4,10,512]{4,2,3,1,0:T(4,128)S(1)}, f32[3,3,4,10,512]{4,2,3,1,0:T(4,128)S(1)}, u32[]{:S(2)}, u32[]{:S(2)}) collective-permute-start(f32[3,3,4,10,512]{4,2,3,1,0:T(4,128)S(1)} %collective-permute-done.6), channel_id=1, source_target_pairs={{0,1},{1,2},{2,3},{3,4},{4,5},{5,6},{6,7},{7,8},{8,9},{9,10},{10,1... | collective-permute-start | bytes 2211848 | tf_op jit(solution)/shard_map/ppermute | solution.py:100
  69.1 13.6 %collective-permute-start.8 = (f32[3,3,4,10,512]{4,2,3,1,0:T(4,128)S(1)}, f32[3,3,4,10,512]{4,2,3,1,0:T(4,128)S(1)}, u32[]{:S(2)}, u32[]{:S(2)}) collective-permute-start(f32[3,3,4,10,512]{4,2,3,1,0:T(4,128)S(1)} %collective-permute-done.7), channel_id=1, source_target_pairs={{0,1},{1,2},{2,3},{3,4},{4,5},{5,6},{6,7},{7,8},{8,9},{9,10},{10,1... | collective-permute-start | bytes 2211848 | tf_op jit(solution)/shard_map/ppermute | solution.py:100
  82.6 127.4 %copy-start.7 = (f32[3,3,4,10,512]{4,2,3,1,0:T(4,128)}, f32[3,3,4,10,512]{4,2,3,1,0:T(4,128)S(1)}, u32[]{:S(2)}) copy-start(f32[3,3,4,10,512]{4,2,3,1,0:T(4,128)S(1)} %collective-permute-done.8) | copy-start | bytes 2211844
  82.6 13.6 %collective-permute-start.9 = (f32[3,3,4,10,512]{4,2,3,1,0:T(4,128)S(1)}, f32[3,3,4,10,512]{4,2,3,1,0:T(4,128)S(1)}, u32[]{:S(2)}, u32[]{:S(2)}) collective-permute-start(f32[3,3,4,10,512]{4,2,3,1,0:T(4,128)S(1)} %collective-permute-done.8), channel_id=1, source_target_pairs={{0,1},{1,2},{2,3},{3,4},{4,5},{5,6},{6,7},{7,8},{8,9},{9,10},{10,1... | collective-permute-start | bytes 2211848 | tf_op jit(solution)/shard_map/ppermute | solution.py:100
  97.1 13.6 %collective-permute-start.10 = (f32[3,3,4,10,512]{4,2,3,1,0:T(4,128)S(1)}, f32[3,3,4,10,512]{4,2,3,1,0:T(4,128)S(1)}, u32[]{:S(2)}, u32[]{:S(2)}) collective-permute-start(f32[3,3,4,10,512]{4,2,3,1,0:T(4,128)S(1)} %collective-permute-done.9), channel_id=1, source_target_pairs={{0,1},{1,2},{2,3},{3,4},{4,5},{5,6},{6,7},{7,8},{8,9},{9,10},{10,1... | collective-permute-start | bytes 2211848 | tf_op jit(solution)/shard_map/ppermute | solution.py:100
  111.5 13.6 %collective-permute-start.11 = (f32[3,3,4,10,512]{4,2,3,1,0:T(4,128)S(1)}, f32[3,3,4,10,512]{4,2,3,1,0:T(4,128)S(1)}, u32[]{:S(2)}, u32[]{:S(2)}) collective-permute-start(f32[3,3,4,10,512]{4,2,3,1,0:T(4,128)S(1)} %collective-permute-done.10), channel_id=1, source_target_pairs={{0,1},{1,2},{2,3},{3,4},{4,5},{5,6},{6,7},{7,8},{8,9},{9,10},{10,1... | collective-permute-start | bytes 2211848 | tf_op jit(solution)/shard_map/ppermute | solution.py:100
  126.0 13.6 %collective-permute-start.12 = (f32[3,3,4,10,512]{4,2,3,1,0:T(4,128)S(1)}, f32[3,3,4,10,512]{4,2,3,1,0:T(4,128)S(1)}, u32[]{:S(2)}, u32[]{:S(2)}) collective-permute-start(f32[3,3,4,10,512]{4,2,3,1,0:T(4,128)S(1)} %collective-permute-done.11), channel_id=1, source_target_pairs={{0,1},{1,2},{2,3},{3,4},{4,5},{5,6},{6,7},{7,8},{8,9},{9,10},{10,1... | collective-permute-start | bytes 2211848 | tf_op jit(solution)/shard_map/ppermute | solution.py:100
  140.5 13.6 %collective-permute-start.13 = (f32[3,3,4,10,512]{4,2,3,1,0:T(4,128)S(1)}, f32[3,3,4,10,512]{4,2,3,1,0:T(4,128)S(1)}, u32[]{:S(2)}, u32[]{:S(2)}) collective-permute-start(f32[3,3,4,10,512]{4,2,3,1,0:T(4,128)S(1)} %collective-permute-done.12), channel_id=1, source_target_pairs={{0,1},{1,2},{2,3},{3,4},{4,5},{5,6},{6,7},{7,8},{8,9},{9,10},{10,1... | collective-permute-start | bytes 2211848 | tf_op jit(solution)/shard_map/ppermute | solution.py:100
  155.0 13.6 %collective-permute-start.14 = (f32[3,3,4,10,512]{4,2,3,1,0:T(4,128)S(1)}, f32[3,3,4,10,512]{4,2,3,1,0:T(4,128)S(1)}, u32[]{:S(2)}, u32[]{:S(2)}) collective-permute-start(f32[3,3,4,10,512]{4,2,3,1,0:T(4,128)S(1)} %collective-permute-done.13), channel_id=1, source_target_pairs={{0,1},{1,2},{2,3},{3,4},{4,5},{5,6},{6,7},{7,8},{8,9},{9,10},{10,1... | collective-permute-start | bytes 2211848 | tf_op jit(solution)/shard_map/ppermute | solution.py:100
  168.5 14.5 %copy-start.19 = (f32[3,3,4,10,512]{4,2,3,1,0:T(4,128)}, f32[3,3,4,10,512]{4,2,3,1,0:T(4,128)S(1)}, u32[]{:S(2)}) copy-start(f32[3,3,4,10,512]{4,2,3,1,0:T(4,128)S(1)} %collective-permute-done.14) | copy-start | bytes 2211844
  168.5 13.7 %collective-permute-start.15 = (f32[3,3,4,10,512]{4,2,3,1,0:T(4,128)S(1)}, f32[3,3,4,10,512]{4,2,3,1,0:T(4,128)}, u32[]{:S(2)}, u32[]{:S(2)}) collective-permute-start(f32[3,3,4,10,512]{4,2,3,1,0:T(4,128)S(1)} %collective-permute-done.14), channel_id=1, source_target_pairs={{0,1},{1,2},{2,3},{3,4},{4,5},{5,6},{6,7},{7,8},{8,9},{9,10},{10,1... | collective-permute-start | bytes 2211848 | tf_op jit(solution)/shard_map/ppermute | solution.py:100
  182.2 13.9 %collective-permute-start.16 = (f32[3,3,4,10,512]{4,2,3,1,0:T(4,128)}, f32[3,3,4,10,512]{4,2,3,1,0:T(4,128)}, u32[]{:S(2)}, u32[]{:S(2)}) collective-permute-start(f32[3,3,4,10,512]{4,2,3,1,0:T(4,128)} %collective-permute-done.15), channel_id=1, source_target_pairs={{0,1},{1,2},{2,3},{3,4},{4,5},{5,6},{6,7},{7,8},{8,9},{9,10},{10,1... | collective-permute-start | bytes 2211848 | tf_op jit(solution)/shard_map/ppermute | solution.py:100
  185.5 11.8 %collective-permute-start = (f32[10,4,1,512]{3,2,1,0:T(1,128)S(1)}, f32[10,4,1,512]{3,2,1,0:T(1,128)S(1)}, u32[]{:S(2)}, u32[]{:S(2)}) collective-permute-start(f32[10,4,1,512]{3,2,1,0:T(1,128)S(1)} %get-tuple-element.389), channel_id=1, source_target_pairs={{0,16},{1,17},{2,18},{3,19},{4,20},{5,21},{6,22},{7,23},{8,24},{9,... | collective-permute-start | bytes 245768 | tf_op jit(solution)/shard_map/ppermute | solution.py:14
  187.0 10.3 %collective-permute-start.1 = (f32[10,4,1,512]{3,2,1,0:T(1,128)S(1)}, f32[10,4,1,512]{3,2,1,0:T(1,128)S(1)}, u32[]{:S(2)}, u32[]{:S(2)}) collective-permute-start(f32[10,4,1,512]{3,2,1,0:T(1,128)S(1)} %get-tuple-element.390), channel_id=1, source_target_pairs={{16,0},{17,1},{18,2},{19,3},{20,4},{21,5},{22,6},{23,7},{24,8},{25... | collective-permute-start | bytes 245768 | tf_op jit(solution)/shard_map/ppermute | solution.py:15
  196.1 13.9 %collective-permute-start.17 = (f32[3,3,4,10,512]{4,2,3,1,0:T(4,128)}, f32[3,3,4,10,512]{4,2,3,1,0:T(4,128)}, u32[]{:S(2)}, u32[]{:S(2)}) collective-permute-start(f32[3,3,4,10,512]{4,2,3,1,0:T(4,128)} %collective-permute-done.16), channel_id=1, source_target_pairs={{0,1},{1,2},{2,3},{3,4},{4,5},{5,6},{6,7},{7,8},{8,9},{9,10},{10,1... | collective-permute-start | bytes 2211848 | tf_op jit(solution)/shard_map/ppermute | solution.py:100
  197.2 40.1 %copy-start.5 = (f32[3,3,4,10,512]{4,2,3,1,0:T(4,128)S(1)}, f32[3,3,4,10,512]{4,2,3,1,0:T(4,128)}, u32[]{:S(2)}) copy-start(f32[3,3,4,10,512]{4,2,3,1,0:T(4,128)} %copy-done.4) | copy-start | bytes 2211844
  197.2 40.2 %copy-start.3 = (f32[3,3,4,10,512]{4,2,3,1,0:T(4,128)S(1)}, f32[3,3,4,10,512]{4,2,3,1,0:T(4,128)}, u32[]{:S(2)}) copy-start(f32[3,3,4,10,512]{4,2,3,1,0:T(4,128)} %copy-done.2) | copy-start | bytes 2211844
  197.2 44.6 %copy-start.20 = (f32[3,3,4,10,512]{4,2,3,1,0:T(4,128)S(1)}, f32[3,3,4,10,512]{4,2,3,1,0:T(4,128)}, u32[]{:S(2)}) copy-start(f32[3,3,4,10,512]{4,2,3,1,0:T(4,128)} %copy-done.19) | copy-start | bytes 2211844
  197.2 44.7 %copy-start.18 = (f32[3,3,4,10,512]{4,2,3,1,0:T(4,128)S(1)}, f32[3,3,4,10,512]{4,2,3,1,0:T(4,128)}, u32[]{:S(2)}) copy-start(f32[3,3,4,10,512]{4,2,3,1,0:T(4,128)} %copy-done.17) | copy-start | bytes 2211844
  197.2 44.8 %copy-start.16 = (f32[3,3,4,10,512]{4,2,3,1,0:T(4,128)S(1)}, f32[3,3,4,10,512]{4,2,3,1,0:T(4,128)}, u32[]{:S(2)}) copy-start(f32[3,3,4,10,512]{4,2,3,1,0:T(4,128)} %copy-done.15) | copy-start | bytes 2211844
  197.3 44.9 %copy-start.14 = (f32[3,3,4,10,512]{4,2,3,1,0:T(4,128)S(1)}, f32[3,3,4,10,512]{4,2,3,1,0:T(4,128)}, u32[]{:S(2)}) copy-start(f32[3,3,4,10,512]{4,2,3,1,0:T(4,128)} %copy-done.13) | copy-start | bytes 2211844
  197.3 45.0 %copy-start.12 = (f32[3,3,4,10,512]{4,2,3,1,0:T(4,128)S(1)}, f32[3,3,4,10,512]{4,2,3,1,0:T(4,128)}, u32[]{:S(2)}) copy-start(f32[3,3,4,10,512]{4,2,3,1,0:T(4,128)} %copy-done.11) | copy-start | bytes 2211844
  197.3 45.1 %copy-start.10 = (f32[3,3,4,10,512]{4,2,3,1,0:T(4,128)S(1)}, f32[3,3,4,10,512]{4,2,3,1,0:T(4,128)}, u32[]{:S(2)}) copy-start(f32[3,3,4,10,512]{4,2,3,1,0:T(4,128)} %copy-done.9) | copy-start | bytes 2211844
  210.0 13.8 %collective-permute-start.18 = (f32[3,3,4,10,512]{4,2,3,1,0:T(4,128)}, f32[3,3,4,10,512]{4,2,3,1,0:T(4,128)S(1)}, u32[]{:S(2)}, u32[]{:S(2)}) collective-permute-start(f32[3,3,4,10,512]{4,2,3,1,0:T(4,128)} %collective-permute-done.17), channel_id=1, source_target_pairs={{0,1},{1,2},{2,3},{3,4},{4,5},{5,6},{6,7},{7,8},{8,9},{9,10},{10,1... | collective-permute-start | bytes 2211848 | tf_op jit(solution)/shard_map/ppermute | solution.py:100
  210.9 31.6 %copy-start.8 = (f32[3,3,4,10,512]{4,2,3,1,0:T(4,128)S(1)}, f32[3,3,4,10,512]{4,2,3,1,0:T(4,128)}, u32[]{:S(2)}) copy-start(f32[3,3,4,10,512]{4,2,3,1,0:T(4,128)} %copy-done.7) | copy-start | bytes 2211844
  (8 other events, 7.0 us)
